TPU v7x, 32 devices: a whole 2x2x4 slice. The times are simulated.
32 devices in a mesh: shard: 2 (over y), ctx: 4 (over z), tp: 4 (over x, core).
Axes of the slice: x: 2, y: 2, z: 4, core: 2. Of those that a mesh axis runs over, the one named last changes fastest.
Arguments:
- inputs: bfloat16 [2, 4096, 768], P('shard', 'ctx'), may hold values from -6 to 6
- lengths: int32 [2], P('shard'), may hold values from 1024 to 4096, as said below
- global_blocks: int32 [2, 2], P('shard'), may hold values from 0 to 15, as said below
- random_blocks: int32 [2, 64, 3], P('shard', 'ctx'), may hold values from 0 to 63
- master_blocks: float32 [768, 96, 96], P(('shard', 'ctx', 'tp'))
- outer_vectors: float32 [6, 768], replicated
- inner_biases: float32 [4, 1152], P('tp'), may hold values from -4 to 4
- left_stats: float32 [768, 96, 96], P(('shard', 'ctx', 'tp')), as said below
- right_stats: float32 [768, 96, 96], P(('shard', 'ctx', 'tp')), as said below
- left_roots: float32 [768, 96, 96], P(('shard', 'ctx', 'tp')), as said below
- right_roots: float32 [768, 96, 96], P(('shard', 'ctx', 'tp')), as said below
- cotangent: bfloat16 [2, 4096, 768], P('shard', 'ctx'), may hold values from -6 to 6
Outputs:
- output: bfloat16 [2, 4096, 768], P('shard', 'ctx')
- input_grad: bfloat16 [2, 4096, 768], P('shard', 'ctx')
- block_grads: float32 [768, 96, 96], P(('shard', 'ctx', 'tp'))
- outer_grads: float32 [6, 768], P(None, ('shard', 'ctx'))
- inner_grads: float32 [4, 1152], P('tp', ('shard', 'ctx'))
- maxima: float32 [12], P('tp')
- left_new: float32 [768, 96, 96], P(('shard', 'ctx', 'tp'))
- right_new: float32 [768, 96, 96], P(('shard', 'ctx', 'tp'))
- new_blocks: float32 [768, 96, 96], P(('shard', 'ctx', 'tp'))
- new_outer: float32 [6, 768], P(None, ('shard', 'ctx'))
- new_inner: float32 [4, 1152], P('tp', ('shard', 'ctx'))
Inputs may be any that keep to these rules, and one draw needn't show every extreme that they name: `lengths`: sequence 0 holds 4096 valid tokens. `global_blocks`: the two ids of a sequence differ. `left_stats`: each block is symmetric. `right_stats`: each block is symmetric. `left_roots`: each block is symmetric. `right_roots`: each block is symmetric.
All inputs are finite; a program needn't handle non-finite values.
Results may differ from a plain program's by a relative error of at most 0.018.
Values may be sent and summed in bfloat16 or wider, within the bound.
No kernel may reach another device: no remote copies, remote signals or barrier semaphores. Data moves between devices by JAX's collectives and lax.ppermute only.
A program may use at most 192 MiB of HBM per device.

v0:
```python
import jax
import jax.numpy as jnp
from jax import lax
from jax.sharding import PartitionSpec as P

D = 768
HEADS = 12
HEAD = 64
FF = 3072
BLOCK = 64
SEQ = 4096
PB = 96
eps_norm = 1e-06
tau_clip = 9.0
rate_matrix = 0.3
rate_vector = 0.001
neg_large = -1e30
high = lax.Precision.HIGHEST


def layer_norm(values, gain, shift):
    mean_val = jnp.mean(values, axis=-1, keepdims=True)
    centred = values - mean_val
    var_val = jnp.mean(centred * centred, axis=-1, keepdims=True)
    return centred * lax.rsqrt(var_val + eps_norm) * gain + shift


def gelu_tanh(values):
    return jax.nn.gelu(values, approximate=True)


def to_grid(blocks, row_count, col_count):
    shaped = blocks.reshape(row_count // PB, col_count // PB, PB, PB)
    return shaped.transpose(0, 2, 1, 3).reshape(row_count, col_count)


def from_grid(matrix):
    row_count, col_count = matrix.shape
    shaped = matrix.reshape(row_count // PB, PB, col_count // PB, PB)
    return shaped.transpose(0, 2, 1, 3).reshape(-1, PB, PB)


def unpack_weights(whole, head_cols, unit_count):
    first_end = D // PB * (3 * head_cols // PB)
    second_end = first_end + head_cols // PB * (D // PB)
    third_end = second_end + D // PB * (unit_count // PB)
    return (
        to_grid(whole[:first_end], D, 3 * head_cols),
        to_grid(whole[first_end:second_end], head_cols, D),
        to_grid(whole[second_end:third_end], D, unit_count),
        to_grid(whole[third_end:], unit_count, D),
    )


def block_layout(slot_length, global_ids, random_ids, first_block, rows_blocks, block_count):
    rows = first_block + jnp.arange(rows_blocks, dtype=jnp.int32)
    window = jnp.stack([rows - 1, rows, rows + 1], axis=1)
    globals_row = jnp.broadcast_to(global_ids[None, :], (rows_blocks, 2))
    listed = jnp.concatenate([window, globals_row, random_ids], axis=1)
    inside = (listed >= 0) & (listed < block_count)
    clipped = jnp.clip(listed, 0, block_count - 1)
    key_pos = listed[:, :, None] * BLOCK + jnp.arange(BLOCK, dtype=jnp.int32)[None, None, :]
    key_mask = (inside[:, :, None] & (key_pos < slot_length)).reshape(rows_blocks, -1)
    query_pos = (first_block * BLOCK + jnp.arange(rows_blocks * BLOCK, dtype=jnp.int32)).reshape(
        rows_blocks, BLOCK
    )
    return (clipped, key_mask, query_pos < slot_length)


def pick_blocks(full_rows, clipped, head_count):
    block_count = full_rows.shape[0] // BLOCK
    picked = full_rows.reshape(block_count, BLOCK, -1)[clipped]
    return picked.reshape(clipped.shape[0], clipped.shape[1] * BLOCK, head_count, HEAD)


def attend_scores(query_blocks, key_blocks):
    return jnp.einsum(
        "lqhd,lkhd->lhqk", query_blocks, key_blocks, preferred_element_type=jnp.float32
    ) * HEAD ** (-0.5)


def probs_again(query_blocks, d_out_blocks, key_blocks, value_blocks, key_mask, lse_blk):
    raw_scores = attend_scores(query_blocks, key_blocks)
    probs = jnp.exp(jnp.where(key_mask[:, None, None, :], raw_scores, neg_large) - lse_blk)
    d_probs = jnp.einsum(
        "lqhd,lkhd->lhqk", d_out_blocks, value_blocks, preferred_element_type=jnp.float32
    )
    return (probs, d_probs)


def group_back(
    query_blocks,
    d_out_blocks,
    key_src,
    value_src,
    clipped,
    key_mask,
    lse_blk,
    delta_blk,
    block_count,
):
    rows_blocks, _, heads_here, _ = query_blocks.shape
    head_cols = heads_here * HEAD
    key_blocks = pick_blocks(key_src, clipped, heads_here)
    value_blocks = pick_blocks(value_src, clipped, heads_here)
    probs, d_probs = probs_again(
        query_blocks, d_out_blocks, key_blocks, value_blocks, key_mask, lse_blk
    )
    delta_blk = jnp.sum(probs * d_probs, axis=-1, keepdims=True)
    d_scores = (probs * (d_probs - delta_blk)).astype(jnp.bfloat16)
    d_query = jnp.einsum(
        "lhqk,lkhd->lqhd", d_scores, key_blocks, preferred_element_type=jnp.float32
    ) * HEAD ** (-0.5)
    d_key_blocks = jnp.einsum(
        "lhqk,lqhd->lkhd", d_scores, query_blocks, preferred_element_type=jnp.float32
    ) * HEAD ** (-0.5)
    d_value_blocks = jnp.einsum(
        "lhqk,lqhd->lkhd",
        probs.astype(jnp.bfloat16),
        d_out_blocks,
        preferred_element_type=jnp.float32,
    )
    listed_count = clipped.shape[1]
    d_key_full = (
        jnp.zeros((block_count, BLOCK, head_cols), jnp.float32)
        .at[clipped]
        .add(d_key_blocks.reshape(rows_blocks, listed_count, BLOCK, head_cols))
    )
    d_value_full = (
        jnp.zeros((block_count, BLOCK, head_cols), jnp.float32)
        .at[clipped]
        .add(d_value_blocks.reshape(rows_blocks, listed_count, BLOCK, head_cols))
    )
    return (
        d_query.reshape(-1, head_cols),
        d_key_full.reshape(-1, head_cols),
        d_value_full.reshape(-1, head_cols),
    )


def per_device(
    inputs,
    lengths,
    global_blocks,
    random_blocks,
    master_blocks,
    outer_vectors,
    inner_biases,
    left_stats,
    right_stats,
    left_roots,
    right_roots,
    cotangent,
):
    tensor_count = lax.axis_size("tp")
    owner_count = lax.axis_size(("shard", "ctx"))
    heads_here = HEADS // tensor_count
    head_cols = heads_here * HEAD
    unit_count = FF // tensor_count
    slot_count, ctx_tokens, _ = inputs.shape
    rows_blocks = ctx_tokens // BLOCK
    block_count = SEQ // BLOCK
    ctx_index = lax.axis_index("ctx")
    owner_index = lax.axis_index(("shard", "ctx"))
    gathered = lax.all_gather(
        master_blocks.astype(jnp.bfloat16), ("shard", "ctx"), axis=0, tiled=True
    )
    w_qkv, w_out, w_up, w_down = unpack_weights(gathered, head_cols, unit_count)
    flat_in = inputs.reshape(-1, D)
    inner_row = inner_biases[0]
    q_bias = inner_row[:head_cols]
    v_bias = inner_row[head_cols : 2 * head_cols]
    up_bias = inner_row[2 * head_cols :]
    projected = jnp.dot(flat_in, w_qkv, preferred_element_type=jnp.float32)
    queries = (projected[:, :head_cols] + q_bias).astype(jnp.bfloat16)
    key_rows = (
        projected[:, head_cols : 2 * head_cols]
        .astype(jnp.bfloat16)
        .reshape(slot_count, ctx_tokens, head_cols)
    )
    value_rows = (
        (projected[:, 2 * head_cols :] + v_bias)
        .astype(jnp.bfloat16)
        .reshape(slot_count, ctx_tokens, head_cols)
    )
    keys_all, values_all = (
        lax.all_gather(key_rows, "ctx", axis=1, tiled=True),
        lax.all_gather(value_rows, "ctx", axis=1, tiled=True),
    )
    query_slots = queries.reshape(slot_count, ctx_tokens, head_cols)
    peak_logit = jnp.full((heads_here,), neg_large, jnp.float32)
    slot_index = 0
    clipped, key_mask, query_mask = block_layout(
        lengths[slot_index],
        global_blocks[slot_index],
        random_blocks[slot_index],
        ctx_index * rows_blocks,
        rows_blocks,
        block_count,
    )
    layouts = [(clipped, key_mask)]
    query_blocks = query_slots[slot_index].reshape(rows_blocks, BLOCK, heads_here, HEAD)
    key_blocks = pick_blocks(keys_all[slot_index], clipped, heads_here)
    value_blocks = pick_blocks(values_all[slot_index], clipped, heads_here)
    raw_scores = attend_scores(query_blocks, key_blocks)
    both_mask = key_mask[:, None, None, :] & query_mask[:, None, :, None]
    peak_logit = jnp.maximum(
        peak_logit, jnp.max(jnp.where(both_mask, raw_scores, neg_large), axis=(0, 2, 3))
    )
    masked = jnp.where(key_mask[:, None, None, :], raw_scores, neg_large)
    row_top = jnp.max(masked, axis=-1, keepdims=True)
    shifted = jnp.exp(masked - row_top)
    row_total = jnp.sum(shifted, axis=-1, keepdims=True)
    probs = shifted / row_total
    lse_list = [row_top + jnp.log(row_total)]
    attended = jnp.einsum(
        "lhqk,lkhd->lqhd",
        probs.astype(jnp.bfloat16),
        value_blocks,
        preferred_element_type=jnp.float32,
    )
    attended_list = attended.reshape(ctx_tokens, head_cols)
    attended_low = attended_list.astype(jnp.bfloat16)
    branch = (
        lax.psum(jnp.dot(attended_low, w_out, preferred_element_type=jnp.float32), "tp")
        + outer_vectors[0]
    )
    hidden_in = flat_in.astype(jnp.float32) + branch
    x_first = layer_norm(hidden_in, outer_vectors[2], outer_vectors[3])
    x_first_low = x_first.astype(jnp.bfloat16)
    gate_pre = jnp.dot(x_first_low, w_up, preferred_element_type=jnp.float32) + up_bias
    act_low = gelu_tanh(gate_pre).astype(jnp.bfloat16)
    ff_out = (
        lax.psum(jnp.dot(act_low, w_down, preferred_element_type=jnp.float32), "tp")
        + outer_vectors[1]
    )
    mixed_sum = x_first + ff_out
    result = layer_norm(mixed_sum, outer_vectors[4], outer_vectors[5])
    maxima = lax.pmax(peak_logit, ("shard", "ctx"))
    positions = ctx_index * ctx_tokens + jnp.arange(ctx_tokens, dtype=jnp.int32)
    row_valid = (positions[None, :] < lengths[:, None]).astype(jnp.float32).reshape(-1)
    d_result = cotangent.reshape(-1, D).astype(jnp.float32) * row_valid[:, None]
    regathered = lax.all_gather(
        master_blocks.astype(jnp.bfloat16), ("shard", "ctx"), axis=0, tiled=True
    )
    wb_qkv, wb_out, wb_up, wb_down = unpack_weights(regathered, head_cols, unit_count)
    _, back_second = jax.vjp(layer_norm, mixed_sum, outer_vectors[4], outer_vectors[5])
    d_mixed, d_gain2, d_shift2 = back_second(d_result)
    d_ff_low = d_mixed.astype(jnp.bfloat16)
    d_bias2 = jnp.sum(d_ff_low.astype(jnp.float32), axis=0)
    g_down = jnp.dot(act_low.T, d_ff_low, preferred_element_type=jnp.float32)
    d_act = jnp.dot(d_ff_low, wb_down.T, preferred_element_type=jnp.float32)
    _, back_gelu = jax.vjp(gelu_tanh, gate_pre)
    d_gate_low = back_gelu(d_act)[0].astype(jnp.bfloat16)
    d_upbias = jnp.sum(d_gate_low.astype(jnp.float32), axis=0)
    g_up = jnp.dot(x_first_low.T, d_gate_low, preferred_element_type=jnp.float32)
    d_first = d_mixed + lax.psum(
        jnp.dot(d_gate_low, wb_up.T, preferred_element_type=jnp.float32), "tp"
    )
    _, back_first = jax.vjp(layer_norm, hidden_in, outer_vectors[2], outer_vectors[3])
    d_hidden, d_gain1, d_shift1 = back_first(d_first)
    d_branch_low = d_hidden.astype(jnp.bfloat16)
    d_bias_out = jnp.sum(d_branch_low.astype(jnp.float32), axis=0)
    g_out = jnp.dot(attended_low.T, d_branch_low, preferred_element_type=jnp.float32)
    d_att_low = jnp.dot(d_branch_low, wb_out.T, preferred_element_type=jnp.float32).astype(
        jnp.bfloat16
    )
    d_att_slots = d_att_low.reshape(slot_count, ctx_tokens, head_cols)
    keys_back, values_back = (keys_all, values_all)
    slot_index = 0
    clipped, key_mask = layouts[slot_index]
    query_blocks = query_slots[slot_index].reshape(rows_blocks, BLOCK, heads_here, HEAD)
    d_out_blocks = d_att_slots[slot_index].reshape(rows_blocks, BLOCK, heads_here, HEAD)
    d_query, d_key_full, d_value_full = group_back(
        query_blocks,
        d_out_blocks,
        keys_back[slot_index],
        values_back[slot_index],
        clipped,
        key_mask,
        lse_list[slot_index],
        None,
        block_count,
    )
    dk_list = [d_key_full]
    dv_list = [d_value_full]
    d_keys, d_values = (
        lax.psum_scatter(
            jnp.stack(dk_list).astype(jnp.bfloat16), "ctx", scatter_dimension=1, tiled=True
        ).astype(jnp.float32),
        lax.psum_scatter(
            jnp.stack(dv_list).astype(jnp.bfloat16), "ctx", scatter_dimension=1, tiled=True
        ).astype(jnp.float32),
    )
    d_q_low = d_query.astype(jnp.bfloat16)
    d_k_low = d_keys.reshape(-1, head_cols).astype(jnp.bfloat16)
    d_v_low = d_values.reshape(-1, head_cols).astype(jnp.bfloat16)
    d_proj = jnp.concatenate([d_q_low, d_k_low, d_v_low], axis=1)
    d_qbias = jnp.sum(d_q_low.astype(jnp.float32), axis=0)
    d_vbias = jnp.sum(d_v_low.astype(jnp.float32), axis=0)
    g_qkv = jnp.dot(flat_in.T, d_proj, preferred_element_type=jnp.float32)
    d_inputs = d_hidden + lax.psum(
        jnp.dot(d_proj, wb_qkv.T, preferred_element_type=jnp.float32).astype(jnp.bfloat16), "tp"
    ).astype(jnp.float32)
    input_grad = d_inputs.reshape(inputs.shape).astype(jnp.bfloat16)
    blocks_grad = jnp.concatenate(
        [from_grid(g_qkv), from_grid(g_out), from_grid(g_up), from_grid(g_down)], axis=0
    )
    outer_part = jnp.stack([d_bias_out, d_bias2, d_gain1, d_shift1, d_gain2, d_shift2], axis=0)
    inner_part = jnp.concatenate([d_qbias, d_vbias, d_upbias])[None, :]
    block_sum, outer_sum, inner_sum = (
        lax.psum_scatter(blocks_grad, ("shard", "ctx"), scatter_dimension=0, tiled=True),
        lax.psum_scatter(outer_part, ("shard", "ctx"), scatter_dimension=1, tiled=True),
        lax.psum_scatter(inner_part, ("shard", "ctx"), scatter_dimension=1, tiled=True),
    )
    left_new = 0.5 * left_stats + 0.5 * jnp.einsum(
        "bij,bkj->bik", block_sum, block_sum, precision=high
    )
    right_new = 0.5 * right_stats + 0.5 * jnp.einsum(
        "bji,bjk->bik", block_sum, block_sum, precision=high
    )
    left_applied = jnp.einsum("bij,bjk->bik", left_roots, block_sum, precision=high)
    step_val = jnp.einsum("bij,bjk->bik", left_applied, right_roots, precision=high)
    clip_sqrt = jnp.sqrt(tau_clip / jnp.maximum(maxima, tau_clip))
    head_factor = jnp.repeat(clip_sqrt, HEAD)
    table = jnp.concatenate([head_factor, head_factor, jnp.ones((head_cols,), jnp.float32)])
    qkv_factor = jnp.tile(table.reshape(1, -1, PB), (D // PB, 1, 1)).reshape(-1, PB)
    blocks_here = master_blocks.shape[0]
    all_factor = jnp.concatenate(
        [qkv_factor, jnp.ones((blocks_here * owner_count - qkv_factor.shape[0], PB), jnp.float32)],
        axis=0,
    )
    own_factor = lax.dynamic_slice_in_dim(all_factor, owner_index * blocks_here, blocks_here, 0)
    new_blocks = (master_blocks - rate_matrix * step_val) * own_factor[:, None, :]
    outer_cols = D // owner_count
    own_outer = lax.dynamic_slice_in_dim(outer_vectors, owner_index * outer_cols, outer_cols, 1)
    new_outer = own_outer - rate_vector * outer_sum
    inner_cols = inner_biases.shape[1] // owner_count
    inner_factor = jnp.concatenate([head_factor, jnp.ones((head_cols + unit_count,), jnp.float32)])
    own_inner_factor = lax.dynamic_slice_in_dim(
        inner_factor, owner_index * inner_cols, inner_cols, 0
    )
    own_inner = lax.dynamic_slice_in_dim(inner_biases, owner_index * inner_cols, inner_cols, 1)
    new_inner = (own_inner - rate_vector * inner_sum) * own_inner_factor[None, :]
    output = result.reshape(inputs.shape).astype(jnp.bfloat16)
    return (
        output,
        input_grad,
        block_sum,
        outer_sum,
        inner_sum,
        maxima,
        left_new,
        right_new,
        new_blocks,
        new_outer,
        new_inner,
    )


def solution(mesh):
    return jax.shard_map(
        per_device,
        mesh=mesh,
        in_specs=(
            P("shard", "ctx", None),
            P("shard"),
            P("shard", None),
            P("shard", "ctx", None),
            P(("shard", "ctx", "tp"), None, None),
            P(),
            P("tp", None),
            P(("shard", "ctx", "tp"), None, None),
            P(("shard", "ctx", "tp"), None, None),
            P(("shard", "ctx", "tp"), None, None),
            P(("shard", "ctx", "tp"), None, None),
            P("shard", "ctx", None),
        ),
        out_specs=(
            P("shard", "ctx", None),
            P("shard", "ctx", None),
            P(("shard", "ctx", "tp"), None, None),
            P(None, ("shard", "ctx")),
            P("tp", ("shard", "ctx")),
            P("tp"),
            P(("shard", "ctx", "tp"), None, None),
            P(("shard", "ctx", "tp"), None, None),
            P(("shard", "ctx", "tp"), None, None),
            P(None, ("shard", "ctx")),
            P("tp", ("shard", "ctx")),
        ),
        check_vma=False,
    )
```

profile of v0, /device:TPU:0, one launch (start us, length us, event | category | flops | bytes accessed | tf_op | source)
XLA Modules:
  0.0 1027.7 jit_solution(3224889106006550222)
XLA Ops:
  9.6 83.2 %all-gather.6.cloned.1.call-done = bf16[192,96,96]{2,1,0:T(8,128)(2,1)} async-done(((bf16[24,96,96]{2,1,0:T(8,128)(2,1)}), bf16[192,96,96]{2,1,0:T(8,128)(2,1)}) %all-gather.6.cloned.1.call-update) | async-done | bytes 3538960 | tf_op jit(solution)/shard_map/all_gather | solution.py:165
  95.8 2.8 fusion.29
  109.1 27.4 %all-gather.10.cloned.1.call-done = bf16[4096,192]{0,1:T(8,128)(2,1)} async-done(((bf16[1024,192]{0,1:T(8,128)(2,1)}), bf16[4096,192]{0,1:T(8,128)(2,1)}) %all-gather.10.cloned.1.call-update) | async-done | bytes 1572880 | tf_op jit(solution)/shard_map/all_gather | solution.py:187
  136.5 3.1 copy.103
  139.7 2.7 gather_fusion.1
  142.4 15.9 %reshape.559 = bf16[16,512,3,64]{3,2,1,0:T(4,128)(2,1)} reshape(bf16[128,64,192]{2,1,0:T(8,128)(2,1)} %gather_fusion.1) | data formatting | bytes 6291456 | tf_op jit(solution)/shard_map/reshape | solution.py:73
  158.4 12.2 %copy.106 = bf16[16,512,3,64]{1,3,2,0:T(8,128)(2,1)} copy(bf16[16,512,3,64]{3,2,1,0:T(4,128)(2,1)} %reshape.559) | data formatting | bytes 6291456 | tf_op jit(solution)/shard_map/reshape | solution.py:73
  170.6 4.1 all-gather.8.cloned.1.call-done
  174.6 3.1 copy.98
  177.8 2.7 gather_fusion
  180.5 15.9 %reshape.558 = bf16[16,512,3,64]{3,2,1,0:T(4,128)(2,1)} reshape(bf16[128,64,192]{2,1,0:T(8,128)(2,1)} %gather_fusion) | data formatting | bytes 6291456 | tf_op jit(solution)/shard_map/reshape | solution.py:73
  196.4 12.3 %copy.107 = bf16[16,512,3,64]{1,3,2,0:T(8,128)(2,1)} copy(bf16[16,512,3,64]{3,2,1,0:T(4,128)(2,1)} %reshape.558) | data formatting | bytes 6291456 | tf_op jit(solution)/shard_map/reshape | solution.py:73
  208.7 3.2 fusion.24
  212.0 3.6 select_reduce_fusion
  216.2 2.7 fusion.39
  227.7 3.8 reshape.488
  233.3 3.9 reshape.490
  237.2 52.6 %all-reduce.7.cloned.1.call-done = f32[1024,768]{1,0:T(8,128)} async-done(((f32[1024,768]{1,0:T(8,128)}), f32[1024,768]{1,0:T(8,128)}) %all-reduce.7.cloned.1.call-update) | async-done | bytes 3145744 | tf_op jit(solution)/shard_map/psum | solution.py:225
  289.8 2.4 fusion.64
  297.7 3.8 fusion.59
  302.4 67.8 %all-reduce.9.cloned.1.call-done = f32[1024,768]{1,0:T(8,128)} async-done(((f32[1024,768]{1,0:T(8,128)}), f32[1024,768]{1,0:T(8,128)}) %all-reduce.9.cloned.1.call-update) | async-done | bytes 3145744 | tf_op jit(solution)/shard_map/psum | solution.py:234
  370.2 3.9 fusion.63
  377.8 2.8 fusion.62
  381.5 2.6 copy-done.76
  384.2 4.3 convert_reduce_fusion
  389.6 3.1 fusion.69
  393.6 67.9 %all-reduce.11.cloned.1.call-done = f32[1024,768]{1,0:T(8,128)} async-done(((f32[1024,768]{1,0:T(8,128)}), f32[1024,768]{1,0:T(8,128)}) %all-reduce.11.cloned.1.call-update) | async-done | bytes 3145744 | tf_op jit(solution)/shard_map/psum | solution.py:257
  461.5 5.4 multiply_reduce_fusion.1
  473.4 7.2 fusion.20
  480.6 15.1 %copy.136 = f32[16,512,3,64]{3,2,1,0:T(4,128)} copy(f32[16,512,3,64]{1,3,2,0:T(8,128)} %fusion.20) | data formatting | bytes 12582912 | tf_op jit(solution)/shard_map/reshape | solution.py:132
  495.7 18.9 %reshape.553 = f32[128,64,192]{2,1,0:T(8,128)} reshape(f32[16,512,3,64]{3,2,1,0:T(4,128)} %copy.136) | data formatting | bytes 12582912 | tf_op jit(solution)/shard_map/reshape | solution.py:132
  514.6 2.5 broadcast.358.clone
  517.0 26.2 %scatter_fusion.1 = f32[64,64,192]{2,1,0:T(8,128)} fusion(f32[64,64,192]{2,1,0:T(8,128)} %broadcast.358.clone, s32[128]{0:T(128)S(1)} %reshape.508, f32[128,64,192]{2,1,0:T(8,128)} %reshape.553), kind=kCustom, calls=%fused_computation.3 | custom fusion | flops 1572864 | bytes 18874880 | tf_op jit(solution)/shard_map/scatter-add | solution.py:132
  543.2 2.5 convert_element_type.178
  545.7 2.7 copy.123
  548.7 6.7 multiply_reduce_fusion
  555.4 3.9 multiply_convert_fusion
  560.9 3.6 multiply_bitcast_fusion
  564.5 15.1 %copy.135 = f32[16,512,3,64]{3,2,1,0:T(4,128)} copy(f32[16,512,3,64]{1,3,2,0:T(8,128)} %multiply_bitcast_fusion) | data formatting | bytes 12582912 | tf_op jit(solution)/shard_map/reshape | solution.py:127
  579.6 18.9 %reshape.552 = f32[128,64,192]{2,1,0:T(8,128)} reshape(f32[16,512,3,64]{3,2,1,0:T(4,128)} %copy.135) | data formatting | bytes 12582912 | tf_op jit(solution)/shard_map/reshape | solution.py:127
  598.5 2.5 broadcast.358.clone.1
  601.0 26.2 %scatter_fusion = f32[64,64,192]{2,1,0:T(8,128)} fusion(f32[64,64,192]{2,1,0:T(8,128)} %broadcast.358.clone.1, s32[128]{0:T(128)S(1)} %reshape.508, f32[128,64,192]{2,1,0:T(8,128)} %reshape.552), kind=kCustom, calls=%fused_computation.2 | custom fusion | flops 1572864 | bytes 18874880 | tf_op jit(solution)/shard_map/scatter-add | solution.py:127
  627.1 2.5 convert_element_type.174
  629.6 2.8 copy.119
  632.7 4.3 fusion.58
  637.0 2.6 reshape.498
  639.5 4.3 copy.127
  645.3 2.6 reshape.496
  647.8 4.3 copy.126
  664.6 3.4 reduce-scatter.10.cloned.1.call-done
  668.0 4.1 convolution_convert_fusion
  674.1 2.7 fusion.31
  676.8 2.4 reshape.493
  681.3 7.7 pad_maximum_fusion
  689.7 19.4 %pmax.7 = f32[3]{0:T(128)S(1)} all-reduce(f32[3]{0:T(128)S(1)} %broadcast_maximum_fusion), channel_id=1, replica_groups=mesh['shard'=2,'ctx'=4,'tp'=4] {'shard','ctx'}, use_global_device_ids=true, to_apply=%region_32.33 | all-reduce | flops 3 | bytes 24 | tf_op jit(solution)/shard_map/pmax | solution.py:239
  710.0 22.3 %reduce-scatter.16.cloned.1.call-done = f32[96,6]{1,0:T(8,128)} async-done(((f32[768,6]{1,0:T(8,128)}), f32[96,6]{1,0:T(8,128)}) %reduce-scatter.16.cloned.1.call-update) | async-done | bytes 2320
  734.6 63.3 %reduce-scatter.18.cloned.1.call-done = f32[144,1]{1,0:T(8,128)} async-done(((f32[1152,1]{1,0:T(8,128)}), f32[144,1]{1,0:T(8,128)}) %reduce-scatter.18.cloned.1.call-update) | async-done | bytes 592
  800.1 42.6 %all-reduce.13.cloned.1.call-done = bf16[1024,768]{1,0:T(8,128)(2,1)} async-done(((bf16[1024,768]{1,0:T(8,128)(2,1)}), bf16[1024,768]{1,0:T(8,128)(2,1)}) %all-reduce.13.cloned.1.call-update) | async-done | bytes 1572880 | tf_op jit(solution)/shard_map/psum | solution.py:302
  842.7 3.9 fusion.26
  846.7 162.3 %reduce-scatter.14.cloned.1.call-done = f32[24,96,96]{2,1,0:T(8,128)} async-done(((f32[192,96,96]{2,1,0:T(8,128)}), f32[24,96,96]{2,1,0:T(8,128)}) %reduce-scatter.14.cloned.1.call-update) | async-done | bytes 884752 | tf_op jit(solution)/shard_map/reduce_scatter | solution.py:312
  1008.9 2.5 fusion.72
  1011.5 2.4 fusion.35
  1013.9 3.2 fusion.36
  1017.0 3.6 fusion.37
  (285 shorter events, 71.4 us)
Async XLA Ops:
  7.2 1001.7 %copy-start = (f32[24,96,96]{2,1,0:T(8,128)S(1)}, f32[24,96,96]{2,1,0:T(8,128)}, u32[]{:S(2)}) copy-start(f32[24,96,96]{2,1,0:T(8,128)} %param.21) | copy-start | bytes 2654212
  7.2 85.6 %all-gather.6.cloned.1.call-start = ((), (), s32[]{:S(2)}) async-start(), calls=%async_computation.5 | async-start | bytes 5308416 | tf_op jit(solution)/shard_map/all_gather | solution.py:165
  9.5 127.0 %all-gather.10.cloned.1.call-start = ((), (), s32[]{:S(2)}) async-start(), calls=%async_computation.14 | async-start | bytes 1966080 | tf_op jit(solution)/shard_map/all_gather | solution.py:187
  95.8 5.2 copy-start.65
  95.8 5.2 copy-start.64
  100.1 3.5 copy-start.73
  100.9 6.9 slice-start.1
  101.0 73.7 %all-gather.8.cloned.1.call-start = ((), (), s32[]{:S(2)}) async-start(), calls=%async_computation.13 | async-start | bytes 1966080 | tf_op jit(solution)/shard_map/all_gather | solution.py:188
  103.4 186.4 %all-reduce.7.cloned.1.call-start = ((), (), s32[]{:S(2)}) async-start(), calls=%async_computation.6 | async-start | bytes 6291456 | tf_op jit(solution)/shard_map/psum | solution.py:225
  196.4 12.3 %copy-start.12 = (bf16[16,64,3,64]{1,0,3,2:T(8,128)(2,1)S(1)}, bf16[16,64,3,64]{1,0,3,2:T(8,128)(2,1)}, u32[]{:S(2)}) copy-start(bf16[16,64,3,64]{1,0,3,2:T(8,128)(2,1)} %reshape_squeeze_reshape.7) | copy-start | bytes 1179652
  208.7 3.3 copy-start.21
  211.9 3.7 copy-start.1
  212.0 3.7 copy-start.37
  212.0 4.2 copy-start.7
  216.2 3.8 copy-start.32
  220.0 3.2 copy-start.52
  222.3 147.8 %all-reduce.9.cloned.1.call-start = ((), (), s32[]{:S(2)}) async-start(), calls=%async_computation.7 | async-start | bytes 6291456 | tf_op jit(solution)/shard_map/psum | solution.py:234
  223.9 68.9 %copy-start.43 = (f32[768]{0:T(1024)}, f32[768]{0:T(1024)S(1)}, u32[]{:S(2)}) copy-start(f32[768]{0:T(1024)S(1)} %get-tuple-element.22) | copy-start | bytes 9220
  223.9 68.9 %copy-start.49 = (f32[768]{0:T(1024)}, f32[768]{0:T(1024)S(1)}, u32[]{:S(2)}) copy-start(f32[768]{0:T(1024)S(1)} %get-tuple-element.21) | copy-start | bytes 9220
  233.3 56.5 %copy-start.23 = (bf16[1,1024,768]{2,1,0:T(8,128)(2,1)S(1)}, bf16[1,1024,768]{2,1,0:T(8,128)(2,1)}, u32[]{:S(2)}) copy-start(bf16[1,1024,768]{2,1,0:T(8,128)(2,1)} %param.12) | copy-start | bytes 4718596
  294.6 3.1 copy-start.31
  294.6 3.1 copy-start.69
  301.5 160.0 %all-reduce.11.cloned.1.call-start = ((), (), s32[]{:S(2)}) async-start(), calls=%async_computation.8 | async-start | bytes 6291456 | tf_op jit(solution)/shard_map/psum | solution.py:257
  374.6 3.1 copy-start.55
  380.6 7.9 copy-start.5
  380.6 3.6 copy-start.76
  380.6 7.9 copy-start.45
  381.5 7.0 copy-start.26
  392.8 68.7 %copy-start.42 = (f32[1024]{0:T(1024)S(1)}, f32[1024]{0:T(1024)}, u32[]{:S(2)}) copy-start(f32[1024]{0:T(1024)} %copy-done.41) | copy-start | bytes 12292
  392.8 68.7 %copy-start.44 = (f32[768]{0:T(1024)S(1)}, f32[768]{0:T(1024)}, u32[]{:S(2)}) copy-start(f32[768]{0:T(1024)} %copy-done.43) | copy-start | bytes 9220
  392.8 68.7 %copy-start.46 = (f32[1024]{0:T(1024)S(1)}, f32[1024]{0:T(1024)}, u32[]{:S(2)}) copy-start(f32[1024]{0:T(1024)} %copy-done.45) | copy-start | bytes 12292
  392.8 269.5 %reduce-scatter.12.cloned.1.call-start = ((), (), s32[]{:S(2)}) async-start(), calls=%async_computation.10 | async-start | bytes 1966080 | tf_op jit(solution)/shard_map/reduce_scatter | solution.py:291
  393.6 73.3 %copy-start.51 = (f32[1024]{0:T(1024)S(1)}, f32[1024]{0:T(1024)}, u32[]{:S(2)}) copy-start(f32[1024]{0:T(1024)} %copy-done.50) | copy-start | bytes 12292
  461.5 5.4 copy-start.3
  468.4 3.8 copy-start.33
  473.4 7.2 copy-start.11
  548.4 119.6 %reduce-scatter.10.cloned.1.call-start = ((), (), s32[]{:S(2)}) async-start(), calls=%async_computation.9 | async-start | bytes 1966080 | tf_op jit(solution)/shard_map/reduce_scatter | solution.py:288
  555.4 5.5 copy-start.13
  629.6 3.1 copy-start.71
  632.4 99.9 %reduce-scatter.16.cloned.1.call-start = ((), (), s32[]{:S(2)}) async-start(), calls=%async_computation.15 | async-start | bytes 442368
  639.5 4.3 copy-start.25
  639.5 4.3 copy-start.78
  645.3 6.9 copy-start.56
  647.8 4.9 copy-start.60
  647.8 5.5 copy-start.59
  647.8 6.0 copy-start.9
  647.8 6.0 copy-start.10
  655.7 3.7 copy-start.16
  655.7 5.4 copy-start.57
  655.7 5.4 copy-start.54
  655.7 5.4 copy-start.53
  659.4 4.0 copy-start.67
  659.4 4.0 copy-start.68
  659.4 8.6 copy-start.36
  662.2 135.6 %reduce-scatter.18.cloned.1.call-start = ((), (), s32[]{:S(2)}) async-start(), calls=%async_computation.16 | async-start | bytes 663552
  664.6 178.1 %all-reduce.13.cloned.1.call-start = ((), (), s32[]{:S(2)}) async-start(), calls=%async_computation.11 | async-start | bytes 3145728 | tf_op jit(solution)/shard_map/psum | solution.py:302
  668.0 4.5 copy-start.17
  668.0 4.5 copy-start.20
  672.1 336.8 %reduce-scatter.14.cloned.1.call-start = ((), (), s32[]{:S(2)}) async-start(), calls=%async_computation.12 | async-start | bytes 10616832 | tf_op jit(solution)/shard_map/reduce_scatter | solution.py:312
  733.2 109.5 %copy-start.58 = (f32[6,96]{1,0:T(8,128)}, f32[6,96]{1,0:T(8,128)S(1)}, u32[]{:S(2)}) copy-start(f32[6,96]{1,0:T(8,128)S(1)} %copy.138) | copy-start | bytes 6916
  798.8 43.9 %copy-start.66 = (f32[1,144]{1,0:T(1,128)}, f32[1,144]{1,0:T(1,128)S(1)}, u32[]{:S(2)}) copy-start(f32[1,144]{1,0:T(1,128)S(1)} %copy.140) | copy-start | bytes 1732
  846.7 164.8 %copy-start.18 = (f32[24,96,96]{2,1,0:T(8,128)S(1)}, f32[24,96,96]{2,1,0:T(8,128)}, u32[]{:S(2)}) copy-start(f32[24,96,96]{2,1,0:T(8,128)} %param.16) | copy-start | bytes 2654212
  846.7 164.8 %copy-start.27 = (f32[24,96,96]{2,1,0:T(8,128)S(1)}, f32[24,96,96]{2,1,0:T(8,128)}, u32[]{:S(2)}) copy-start(f32[24,96,96]{2,1,0:T(8,128)} %param.22) | copy-start | bytes 2654212
  1013.9 3.2 copy-start.29
  (29 other events, 42.9 us)
Sparse Core Ops, SparseCore 0:
  10.7 82.0 all-gather.5
  101.1 35.3 all-gather.9
  138.7 35.9 all-gather.7
  222.5 67.2 all-reduce.6
  301.6 68.5 all-reduce.8
  392.9 68.5 all-reduce.10
  548.5 35.4 reduce-scatter.11
  632.5 35.4 reduce-scatter.9
  671.3 61.0 reduce-scatter.15
  736.0 61.7 reduce-scatter.17
  800.8 41.8 all-reduce.12
  846.7 162.1 reduce-scatter.13
where the time goes:
time: 1030 us
  waiting for transfers between devices  597 us (58%)
  local copies, waits for them, and re-layouts  215 us (21%)
  other arithmetic  108 us (10%)
  matrix products  69.6 us (7%)
  blocking collectives  19.4 us (2%)
  between operations  16.1 us (2%)
    reduce_scatter x1, waiting for transfers between devices, per_device(): lax.psum_scatter(blocks_grad, ('shard', 'ctx'), scatter_dimension=0, tile...  162 us
    unnamed x14, waiting for transfers between devices  85.7 us
    all_gather x1, waiting for transfers between devices, per_device(): lax.all_gather(master_blocks.astype(jnp.bfloat16), ('shard', 'ctx'), axis...  83.2 us
    psum x1, waiting for transfers between devices, per_device(): lax.psum(jnp.dot(d_gate_low, wb_up.T, preferred_element_type=jnp.float32)...  67.9 us
    psum x1, waiting for transfers between devices, per_device(): lax.psum(jnp.dot(act_low, w_down, preferred_element_type=jnp.float32), 'tp')  67.8 us
    reshape x4, local copies, waits for them, and re-layouts, pick_blocks(): picked.reshape(clipped.shape[0], clipped.shape[1] * BLOCK, head_count, HEAD)  56.3 us
    psum x1, waiting for transfers between devices, per_device(): lax.psum(jnp.dot(attended_low, w_out, preferred_element_type=jnp.float32)...  52.6 us
    psum x1, waiting for transfers between devices, per_device(): lax.psum(jnp.dot(d_proj, wb_qkv.T, preferred_element_type=jnp.float32).as...  42.6 us
  transfers between devices with their start and end apart: 12, of which 11 were waited for; matrix products, arithmetic and copies ran while one was open for 19% of the time, Pallas kernels for 0%

commit v1 on v0

--- a/solution.py
+++ b/solution.py
@@ -16,6 +16,27 @@
 rate_vector = 0.001
 neg_large = -1e30
 high = lax.Precision.HIGHEST
+
+
+def gather_around(shard, axis, dim):
+    size, index, rows = (lax.axis_size(axis), lax.axis_index(axis), shard.shape[dim])
+    upward = [(i, (i + 1) % size) for i in range(size)]
+    downward = [(i, (i - 1) % size) for i in range(size)]
+    whole = jnp.zeros((*shard.shape[:dim], size * rows, *shard.shape[dim + 1 :]), shard.dtype)
+    whole = lax.dynamic_update_slice_in_dim(whole, shard, index * rows, axis=dim)
+    from_left = from_right = shard
+    middle = size // 2
+    for hop in range(1, middle + 1):
+        from_left = lax.ppermute(from_left, axis, upward)
+        whole = lax.dynamic_update_slice_in_dim(
+            whole, from_left, (index - hop) % size * rows, axis=dim
+        )
+        if hop < size - middle:
+            from_right = lax.ppermute(from_right, axis, downward)
+            whole = lax.dynamic_update_slice_in_dim(
+                whole, from_right, (index + hop) % size * rows, axis=dim
+            )
+    return whole
 
 
 def layer_norm(values, gain, shift):
@@ -184,7 +205,7 @@
         .reshape(slot_count, ctx_tokens, head_cols)
     )
     keys_all, values_all = (
-        lax.all_gather(key_rows, "ctx", axis=1, tiled=True),
+        gather_around(key_rows, "ctx", 1),
         lax.all_gather(value_rows, "ctx", axis=1, tiled=True),
     )
     query_slots = queries.reshape(slot_count, ctx_tokens, head_cols)

time: 1030 us -> 1060 us (1.029)
  local copies, waits for them, and re-layouts: 215 us -> 231 us
  starting transfers between devices: 2.24 us -> 16.5 us
  waiting for transfers between devices: 597 us -> 585 us
    all_gather x1 -> x0, waiting for transfers between devices: 27.4 us -> none  [per_device(): lax.all_gather(key_rows, 'ctx', axis=1, tiled=True)]
    ppermute x0 -> x3, waiting for transfers between devices: none -> 22.9 us  [the longest x2 21.2 us: gather_around(): from_left = lax.ppermute(from_left, axis, upward)]
    ppermute x0 -> x3, starting transfers between devices: none -> 14.5 us  [the longest x2 11.5 us: gather_around(): from_left = lax.ppermute(from_left, axis, upward)]
    unnamed x164 -> x162, local copies, waits for them, and re-layouts: 19.5 us -> 23 us
    unnamed x14 -> x13, waiting for transfers between devices: 85.7 us -> 85.9 us
  transfers between devices with their start and end apart: 12 -> 14, of which waited for: 11 -> 12; matrix products, arithmetic and copies ran while one was open for 19% -> 21% of each run, Pallas kernels for 0% -> 0%
where the time goes in v1:
time: 1060 us; the launch traced here: 1050 us
  waiting for transfers between devices  585 us (55%)
  local copies, waits for them, and re-layouts  231 us (22%)
  other arithmetic  108 us (10%)
  matrix products  72.9 us (7%)
  blocking collectives  19.3 us (2%)
  starting transfers between devices  16.5 us (2%)
  between operations  15.7 us (1%)
    reduce_scatter x1, waiting for transfers between devices, per_device(): lax.psum_scatter(blocks_grad, ('shard', 'ctx'), scatter_dimension=0, tile...  162 us
    unnamed x13, waiting for transfers between devices  85.9 us
    all_gather x1, waiting for transfers between devices, per_device(): lax.all_gather(master_blocks.astype(jnp.bfloat16), ('shard', 'ctx'), axis...  78.2 us
    psum x1, waiting for transfers between devices, per_device(): lax.psum(jnp.dot(d_gate_low, wb_up.T, preferred_element_type=jnp.float32)...  67.9 us
    psum x1, waiting for transfers between devices, per_device(): lax.psum(jnp.dot(act_low, w_down, preferred_element_type=jnp.float32), 'tp')  67.8 us
    reshape x4, local copies, waits for them, and re-layouts, pick_blocks(): picked.reshape(clipped.shape[0], clipped.shape[1] * BLOCK, head_count, HEAD)  56.3 us
    psum x1, waiting for transfers between devices, per_device(): lax.psum(jnp.dot(attended_low, w_out, preferred_element_type=jnp.float32)...  54.7 us
    psum x1, waiting for transfers between devices, per_device(): lax.psum(jnp.dot(d_proj, wb_qkv.T, preferred_element_type=jnp.float32).as...  42.4 us
  transfers between devices with their start and end apart: 14, of which 12 were waited for; matrix products, arithmetic and copies ran while one was open for 21% of the time, Pallas kernels for 0%

profile of v1, /device:TPU:0, one launch (start us, length us, event | category | flops | bytes accessed | tf_op | source)
XLA Modules:
  0.0 1048.5 jit_solution(9021119619010124140)
XLA Ops:
  14.6 78.2 %all-gather.4.cloned.1.call-done = bf16[192,96,96]{2,1,0:T(8,128)(2,1)} async-done(((bf16[24,96,96]{2,1,0:T(8,128)(2,1)}), bf16[192,96,96]{2,1,0:T(8,128)(2,1)}) %all-gather.4.cloned.1.call-update) | async-done | bytes 3538960 | tf_op jit(solution)/shard_map/all_gather | solution.py:186
  95.8 2.8 fusion.29
  104.1 3.0 collective-permute-start.1
  108.2 14.2 %collective-permute-done = bf16[1,1024,192]{1,2,0:T(8,128)(2,1)} collective-permute-done((bf16[1,1024,192]{1,2,0:T(8,128)(2,1)}, bf16[1,1024,192]{1,2,0:T(8,128)(2,1)}, u32[]{:S(2)}, u32[]{:S(2)}) %collective-permute-start) | collective-permute-done | bytes 393248 | tf_op jit(solution)/shard_map/ppermute | solution.py:30
  122.4 10.6 %collective-permute-start.2 = (bf16[1,1024,192]{1,2,0:T(8,128)(2,1)}, bf16[1,1024,192]{1,2,0:T(8,128)(2,1)}, u32[]{:S(2)}, u32[]{:S(2)}) collective-permute-start(bf16[1,1024,192]{1,2,0:T(8,128)(2,1)} %collective-permute-done), channel_id=1, source_target_pairs={{0,4},{4,8},{8,12},{12,0},{1,5},{5,9},{9,13},{13,1},{2,6},{6,10},{... | collective-permute-start | bytes 1179656 | tf_op jit(solution)/shard_map/ppermute | solution.py:30
  146.6 7.0 collective-permute-done.2
  156.7 2.7 gather_fusion.1
  159.4 15.9 %reshape.557 = bf16[16,512,3,64]{3,2,1,0:T(4,128)(2,1)} reshape(bf16[128,64,192]{2,1,0:T(8,128)(2,1)} %gather_fusion.1) | data formatting | bytes 6291456 | tf_op jit(solution)/shard_map/reshape | solution.py:94
  175.3 12.3 %copy.115 = bf16[16,512,3,64]{1,3,2,0:T(8,128)(2,1)} copy(bf16[16,512,3,64]{3,2,1,0:T(4,128)(2,1)} %reshape.557) | data formatting | bytes 6291456 | tf_op jit(solution)/shard_map/reshape | solution.py:94
  187.6 3.2 fusion.24
  190.9 2.7 copy-done.1
  193.6 3.6 select_reduce_fusion
  197.2 3.2 copy.104
  200.4 2.7 gather_fusion
  203.1 15.9 %reshape.556 = bf16[16,512,3,64]{3,2,1,0:T(4,128)(2,1)} reshape(bf16[128,64,192]{2,1,0:T(8,128)(2,1)} %gather_fusion) | data formatting | bytes 6291456 | tf_op jit(solution)/shard_map/reshape | solution.py:94
  219.0 12.2 %copy.116 = bf16[16,512,3,64]{1,3,2,0:T(8,128)(2,1)} copy(bf16[16,512,3,64]{3,2,1,0:T(4,128)(2,1)} %reshape.556) | data formatting | bytes 6291456 | tf_op jit(solution)/shard_map/reshape | solution.py:94
  231.3 6.0 fusion.39
  246.0 3.8 reshape.488
  251.6 3.9 reshape.490
  255.5 54.7 %all-reduce.7.cloned.1.call-done = f32[1024,768]{1,0:T(8,128)} async-done(((f32[1024,768]{1,0:T(8,128)}), f32[1024,768]{1,0:T(8,128)}) %all-reduce.7.cloned.1.call-update) | async-done | bytes 3145744 | tf_op jit(solution)/shard_map/psum | solution.py:246
  318.0 3.8 fusion.62
  322.7 67.8 %all-reduce.9.cloned.1.call-done = f32[1024,768]{1,0:T(8,128)} async-done(((f32[1024,768]{1,0:T(8,128)}), f32[1024,768]{1,0:T(8,128)}) %all-reduce.9.cloned.1.call-update) | async-done | bytes 3145744 | tf_op jit(solution)/shard_map/psum | solution.py:255
  390.5 3.9 fusion.66
  398.1 2.8 fusion.65
  401.8 2.6 copy-done.75
  404.5 4.3 convert_reduce_fusion
  410.0 3.1 fusion.72
  413.9 67.9 %all-reduce.11.cloned.1.call-done = f32[1024,768]{1,0:T(8,128)} async-done(((f32[1024,768]{1,0:T(8,128)}), f32[1024,768]{1,0:T(8,128)}) %all-reduce.11.cloned.1.call-update) | async-done | bytes 3145744 | tf_op jit(solution)/shard_map/psum | solution.py:278
  481.9 5.4 multiply_reduce_fusion.1
  493.8 7.2 fusion.20
  501.0 15.0 %copy.145 = f32[16,512,3,64]{3,2,1,0:T(4,128)} copy(f32[16,512,3,64]{1,3,2,0:T(8,128)} %fusion.20) | data formatting | bytes 12582912 | tf_op jit(solution)/shard_map/reshape | solution.py:153
  516.0 18.9 %reshape.551 = f32[128,64,192]{2,1,0:T(8,128)} reshape(f32[16,512,3,64]{3,2,1,0:T(4,128)} %copy.145) | data formatting | bytes 12582912 | tf_op jit(solution)/shard_map/reshape | solution.py:153
  534.9 2.5 broadcast.361.clone
  537.4 26.5 %scatter_fusion.1 = f32[64,64,192]{2,1,0:T(8,128)} fusion(f32[64,64,192]{2,1,0:T(8,128)} %broadcast.361.clone, s32[128]{0:T(128)S(1)} %reshape.508, f32[128,64,192]{2,1,0:T(8,128)} %reshape.551), kind=kCustom, calls=%fused_computation.3 | custom fusion | flops 1572864 | bytes 18874880 | tf_op jit(solution)/shard_map/scatter-add | solution.py:153
  563.8 2.5 convert_element_type.178
  566.3 2.7 copy.132
  569.3 6.7 multiply_reduce_fusion
  576.0 3.9 multiply_convert_fusion
  581.7 3.6 multiply_bitcast_fusion
  585.3 15.1 %copy.144 = f32[16,512,3,64]{3,2,1,0:T(4,128)} copy(f32[16,512,3,64]{1,3,2,0:T(8,128)} %multiply_bitcast_fusion) | data formatting | bytes 12582912 | tf_op jit(solution)/shard_map/reshape | solution.py:148
  600.4 18.9 %reshape.550 = f32[128,64,192]{2,1,0:T(8,128)} reshape(f32[16,512,3,64]{3,2,1,0:T(4,128)} %copy.144) | data formatting | bytes 12582912 | tf_op jit(solution)/shard_map/reshape | solution.py:148
  619.2 2.5 broadcast.361.clone.1
  621.7 26.5 %scatter_fusion = f32[64,64,192]{2,1,0:T(8,128)} fusion(f32[64,64,192]{2,1,0:T(8,128)} %broadcast.361.clone.1, s32[128]{0:T(128)S(1)} %reshape.508, f32[128,64,192]{2,1,0:T(8,128)} %reshape.550), kind=kCustom, calls=%fused_computation.2 | custom fusion | flops 1572864 | bytes 18874880 | tf_op jit(solution)/shard_map/scatter-add | solution.py:148
  648.2 2.5 convert_element_type.174
  650.7 2.8 copy.128
  653.8 4.3 fusion.61
  658.1 2.6 reshape.498
  660.7 4.3 copy.136
  666.4 2.6 reshape.496
  669.0 4.4 copy.135
  685.9 3.0 reduce-scatter.10.cloned.1.call-done
  688.9 4.1 convolution_convert_fusion
  695.0 2.7 fusion.31
  697.7 2.4 reshape.493
  702.2 7.8 pad_maximum_fusion
  710.6 19.3 %pmax.7 = f32[3]{0:T(128)S(1)} all-reduce(f32[3]{0:T(128)S(1)} %broadcast_maximum_fusion), channel_id=1, replica_groups=mesh['shard'=2,'ctx'=4,'tp'=4] {'shard','ctx'}, use_global_device_ids=true, to_apply=%region_32.33 | all-reduce | flops 3 | bytes 24 | tf_op jit(solution)/shard_map/pmax | solution.py:260
  730.9 22.4 %reduce-scatter.16.cloned.1.call-done = f32[96,6]{1,0:T(8,128)} async-done(((f32[768,6]{1,0:T(8,128)}), f32[96,6]{1,0:T(8,128)}) %reduce-scatter.16.cloned.1.call-update) | async-done | bytes 2320
  755.6 63.3 %reduce-scatter.18.cloned.1.call-done = f32[144,1]{1,0:T(8,128)} async-done(((f32[1152,1]{1,0:T(8,128)}), f32[144,1]{1,0:T(8,128)}) %reduce-scatter.18.cloned.1.call-update) | async-done | bytes 592
  821.2 42.4 %all-reduce.13.cloned.1.call-done = bf16[1024,768]{1,0:T(8,128)(2,1)} async-done(((bf16[1024,768]{1,0:T(8,128)(2,1)}), bf16[1024,768]{1,0:T(8,128)(2,1)}) %all-reduce.13.cloned.1.call-update) | async-done | bytes 1572880 | tf_op jit(solution)/shard_map/psum | solution.py:323
  863.6 3.9 fusion.26
  867.5 162.4 %reduce-scatter.14.cloned.1.call-done = f32[24,96,96]{2,1,0:T(8,128)} async-done(((f32[192,96,96]{2,1,0:T(8,128)}), f32[24,96,96]{2,1,0:T(8,128)}) %reduce-scatter.14.cloned.1.call-update) | async-done | bytes 884752 | tf_op jit(solution)/shard_map/reduce_scatter | solution.py:333
  1029.9 2.5 fusion.75
  1034.9 3.2 fusion.36
  1038.1 3.6 fusion.37
  (294 shorter events, 93.5 us)
Async XLA Ops:
  7.2 1022.8 %copy-start = (f32[24,96,96]{2,1,0:T(8,128)S(1)}, f32[24,96,96]{2,1,0:T(8,128)}, u32[]{:S(2)}) copy-start(f32[24,96,96]{2,1,0:T(8,128)} %param.21) | copy-start | bytes 2654212
  7.2 85.6 %all-gather.4.cloned.1.call-start = ((), (), s32[]{:S(2)}) async-start(), calls=%async_computation.5 | async-start | bytes 5308416 | tf_op jit(solution)/shard_map/all_gather | solution.py:186
  9.5 187.7 %all-gather.6.cloned.1.call-start = ((), (), s32[]{:S(2)}) async-start(), calls=%async_computation.13 | async-start | bytes 1966080 | tf_op jit(solution)/shard_map/all_gather | solution.py:209
  95.8 2.9 copy-start.33
  98.7 5.2 copy-start.71
  100.1 36.2 %slice-start.1 = ((bf16[192,96,96]{2,1,0:T(8,128)(2,1)}), bf16[16,96,96]{2,1,0:T(8,128)(2,1)S(1)}, s32[]{:S(2)}) async-start(bf16[192,96,96]{2,1,0:T(8,128)(2,1)} %all-gather.4.cloned.1.call-done), calls=%async_computation.17 | async-start | bytes 786432 | tf_op jit(solution)/shard_map/slice | solution.py:70
  101.0 209.2 %all-reduce.7.cloned.1.call-start = ((), (), s32[]{:S(2)}) async-start(), calls=%async_computation.6 | async-start | bytes 6291456 | tf_op jit(solution)/shard_map/psum | solution.py:246
  103.0 19.4 %collective-permute-start = (bf16[1,1024,192]{1,2,0:T(8,128)(2,1)}, bf16[1,1024,192]{1,2,0:T(8,128)(2,1)}, u32[]{:S(2)}, u32[]{:S(2)}) collective-permute-start(bf16[1,1024,192]{1,2,0:T(8,128)(2,1)} %fusion.48), channel_id=1, source_target_pairs={{0,4},{4,8},{8,12},{12,0},{1,5},{5,9},{9,13},{13,1},{2,6},{6,10},{... | collective-permute-start | bytes 1179656 | tf_op jit(solution)/shard_map/ppermute | solution.py:30
  104.1 38.3 %collective-permute-start.1 = (bf16[1,1024,192]{1,2,0:T(8,128)(2,1)}, bf16[1,1024,192]{1,2,0:T(8,128)(2,1)}, u32[]{:S(2)}, u32[]{:S(2)}) collective-permute-start(bf16[1,1024,192]{1,2,0:T(8,128)(2,1)} %fusion.48), channel_id=1, source_target_pairs={{0,12},{4,0},{8,4},{12,8},{1,13},{5,1},{9,5},{13,9},{2,14},{6,2},{... | collective-permute-start | bytes 1179656 | tf_op jit(solution)/shard_map/ppermute | solution.py:35
  122.4 31.2 %collective-permute-start.2 = (bf16[1,1024,192]{1,2,0:T(8,128)(2,1)}, bf16[1,1024,192]{1,2,0:T(8,128)(2,1)}, u32[]{:S(2)}, u32[]{:S(2)}) collective-permute-start(bf16[1,1024,192]{1,2,0:T(8,128)(2,1)} %collective-permute-done), channel_id=1, source_target_pairs={{0,4},{4,8},{8,12},{12,0},{1,5},{5,9},{9,13},{13,1},{2,6},{6,10},{... | collective-permute-start | bytes 1179656 | tf_op jit(solution)/shard_map/ppermute | solution.py:30
  175.3 12.3 %copy-start.11 = (bf16[16,64,3,64]{1,0,3,2:T(8,128)(2,1)S(1)}, bf16[16,64,3,64]{1,0,3,2:T(8,128)(2,1)}, u32[]{:S(2)}) copy-start(bf16[16,64,3,64]{1,0,3,2:T(8,128)(2,1)} %reshape_squeeze_reshape.7) | copy-start | bytes 1179652
  187.6 6.0 copy-start.20
  190.9 40.4 %copy-start.36 = (f32[16,3,64]{2,1,0:T(4,128)}, f32[16,3,64]{2,1,0:T(4,128)S(1)}, u32[]{:S(2)}) copy-start(f32[16,3,64]{2,1,0:T(4,128)S(1)} %get-tuple-element.47) | copy-start | bytes 36868
  197.2 34.1 %copy-start.38 = (f32[16,3,64]{2,1,0:T(4,128)}, f32[16,3,64]{2,1,0:T(4,128)S(1)}, u32[]{:S(2)}) copy-start(f32[16,3,64]{2,1,0:T(4,128)S(1)} %get-tuple-element.14) | copy-start | bytes 36868
  231.2 7.0 copy-start.31
  238.3 3.2 copy-start.51
  240.6 149.9 %all-reduce.9.cloned.1.call-start = ((), (), s32[]{:S(2)}) async-start(), calls=%async_computation.7 | async-start | bytes 6291456 | tf_op jit(solution)/shard_map/psum | solution.py:255
  242.1 71.0 %copy-start.42 = (f32[768]{0:T(1024)}, f32[768]{0:T(1024)S(1)}, u32[]{:S(2)}) copy-start(f32[768]{0:T(1024)S(1)} %get-tuple-element.22) | copy-start | bytes 9220
  242.1 71.0 %copy-start.48 = (f32[768]{0:T(1024)}, f32[768]{0:T(1024)S(1)}, u32[]{:S(2)}) copy-start(f32[768]{0:T(1024)S(1)} %get-tuple-element.21) | copy-start | bytes 9220
  251.6 58.6 %copy-start.22 = (bf16[1,1024,768]{2,1,0:T(8,128)(2,1)S(1)}, bf16[1,1024,768]{2,1,0:T(8,128)(2,1)}, u32[]{:S(2)}) copy-start(bf16[1,1024,768]{2,1,0:T(8,128)(2,1)} %param.12) | copy-start | bytes 4718596
  315.0 3.0 copy-start.30
  315.0 3.0 copy-start.67
  321.8 160.0 %all-reduce.11.cloned.1.call-start = ((), (), s32[]{:S(2)}) async-start(), calls=%async_computation.8 | async-start | bytes 6291456 | tf_op jit(solution)/shard_map/psum | solution.py:278
  395.0 3.1 copy-start.54
  400.9 7.9 copy-start.5
  400.9 3.6 copy-start.75
  400.9 7.9 copy-start.44
  401.8 7.0 copy-start.25
  413.1 68.7 %copy-start.41 = (f32[1024]{0:T(1024)S(1)}, f32[1024]{0:T(1024)}, u32[]{:S(2)}) copy-start(f32[1024]{0:T(1024)} %copy-done.40) | copy-start | bytes 12292
  413.1 68.7 %copy-start.43 = (f32[768]{0:T(1024)S(1)}, f32[768]{0:T(1024)}, u32[]{:S(2)}) copy-start(f32[768]{0:T(1024)} %copy-done.42) | copy-start | bytes 9220
  413.1 68.7 %copy-start.45 = (f32[1024]{0:T(1024)S(1)}, f32[1024]{0:T(1024)}, u32[]{:S(2)}) copy-start(f32[1024]{0:T(1024)} %copy-done.44) | copy-start | bytes 12292
  413.2 270.4 %reduce-scatter.12.cloned.1.call-start = ((), (), s32[]{:S(2)}) async-start(), calls=%async_computation.10 | async-start | bytes 1966080 | tf_op jit(solution)/shard_map/reduce_scatter | solution.py:312
  413.9 73.3 %copy-start.50 = (f32[1024]{0:T(1024)S(1)}, f32[1024]{0:T(1024)}, u32[]{:S(2)}) copy-start(f32[1024]{0:T(1024)} %copy-done.49) | copy-start | bytes 12292
  481.9 5.4 copy-start.3
  488.8 3.8 copy-start.32
  493.7 7.3 copy-start.10
  569.1 119.8 %reduce-scatter.10.cloned.1.call-start = ((), (), s32[]{:S(2)}) async-start(), calls=%async_computation.9 | async-start | bytes 1966080 | tf_op jit(solution)/shard_map/reduce_scatter | solution.py:309
  576.0 5.6 copy-start.12
  650.7 3.1 copy-start.69
  653.5 99.8 %reduce-scatter.16.cloned.1.call-start = ((), (), s32[]{:S(2)}) async-start(), calls=%async_computation.14 | async-start | bytes 442368
  660.7 4.3 copy-start.24
  660.7 4.3 copy-start.77
  666.4 7.0 copy-start.55
  669.0 5.0 copy-start.59
  669.0 5.6 copy-start.58
  669.0 6.1 copy-start.8
  669.0 6.1 copy-start.9
  677.0 3.7 copy-start.15
  677.0 5.4 copy-start.56
  677.0 5.4 copy-start.53
  677.0 5.4 copy-start.52
  680.7 4.0 copy-start.65
  680.7 4.0 copy-start.66
  680.7 8.2 copy-start.35
  683.5 135.4 %reduce-scatter.18.cloned.1.call-start = ((), (), s32[]{:S(2)}) async-start(), calls=%async_computation.15 | async-start | bytes 663552
  685.8 177.8 %all-reduce.13.cloned.1.call-start = ((), (), s32[]{:S(2)}) async-start(), calls=%async_computation.11 | async-start | bytes 3145728 | tf_op jit(solution)/shard_map/psum | solution.py:323
  688.9 4.5 copy-start.16
  688.9 4.5 copy-start.19
  693.1 336.9 %reduce-scatter.14.cloned.1.call-start = ((), (), s32[]{:S(2)}) async-start(), calls=%async_computation.12 | async-start | bytes 10616832 | tf_op jit(solution)/shard_map/reduce_scatter | solution.py:333
  754.2 109.4 %copy-start.57 = (f32[6,96]{1,0:T(8,128)}, f32[6,96]{1,0:T(8,128)S(1)}, u32[]{:S(2)}) copy-start(f32[6,96]{1,0:T(8,128)S(1)} %copy.147) | copy-start | bytes 6916
  819.8 43.8 %copy-start.64 = (f32[1,144]{1,0:T(1,128)}, f32[1,144]{1,0:T(1,128)S(1)}, u32[]{:S(2)}) copy-start(f32[1,144]{1,0:T(1,128)S(1)} %copy.149) | copy-start | bytes 1732
  867.5 164.9 %copy-start.17 = (f32[24,96,96]{2,1,0:T(8,128)S(1)}, f32[24,96,96]{2,1,0:T(8,128)}, u32[]{:S(2)}) copy-start(f32[24,96,96]{2,1,0:T(8,128)} %param.16) | copy-start | bytes 2654212
  867.5 164.9 %copy-start.26 = (f32[24,96,96]{2,1,0:T(8,128)S(1)}, f32[24,96,96]{2,1,0:T(8,128)}, u32[]{:S(2)}) copy-start(f32[24,96,96]{2,1,0:T(8,128)} %param.22) | copy-start | bytes 2654212
  1034.9 3.2 copy-start.28
  (30 other events, 45.6 us)
Sparse Core Ops, SparseCore 0:
  10.7 82.0 all-gather.3
  101.1 55.7 all-gather.5
  240.7 69.4 all-reduce.6
  322.0 68.5 all-reduce.8
  413.3 68.5 all-reduce.10
  569.2 35.3 reduce-scatter.11
  653.7 35.1 reduce-scatter.9
  692.2 61.0 reduce-scatter.15
  757.2 61.6 reduce-scatter.17
  821.7 41.8 all-reduce.12
  867.7 162.1 reduce-scatter.13
